TPU v7x, 32 devices: a whole 2x2x4 slice. The times are simulated.
32 devices in a mesh: ens: 2 (over y), wave: 4 (over z), lev: 2 (over x), pot: 2 (over core).
Axes of the slice: x: 2, y: 2, z: 4, core: 2. Of those that a mesh axis runs over, the one named last changes fastest.
Arguments:
- spectra: bfloat16 [4, 64, 2, 64, 512], P(('ens', 'pot'), 'wave', None, 'lev'), parts along dimension 0, may hold values from -0.1875 to 0.1875
- legendre: bfloat16 [64, 768, 512], P('wave', 'lev'), may hold values from -0.25 to 0.25
- row_map: int32 [4, 32], replicated, may hold values from 0 to 767, as said below
- seg_map: int32 [4, 32], replicated, may hold values from 0 to 11
- interp: bfloat16 [4, 32, 128, 128], P('wave'), may hold values from -0.5 to 0.5
- edges: int32 [4, 4, 12288], P('wave'), may hold values from 0 to 4351, as said below
- inv_len: float32 [4, 2, 12288], P('wave'), may hold values from 0.5 to 2
Outputs:
- normal_wind: bfloat16 [128, 49152], P(('ens', 'lev', 'pot'), 'wave'), parts along dimension 0
There are 2 independent parts, one for each index of `ens`. A program takes and returns all parts, laid end to end along the dimension named above; an argument that names none is the same for every part. Nothing has to cross between parts.
Inputs may be any that keep to these rules, and one draw needn't show every extreme that they name: For each patch q and each band b of rows b * 192 to b * 192 + 191, at most 24 entries of row_map[q, :] lie in band b, and every patch has exactly 24 entries in some band. edges[q, 0, e] lies in 128 to 4223, and edges[q, 1, e], edges[q, 2, e], edges[q, 3, e] each lie within 128 of it.
All inputs are finite; a program needn't handle non-finite values.
Results may differ from a plain program's by a relative error of at most 0.0068.
Values may be sent and summed in bfloat16 or wider, within the bound.
No kernel may reach another device: no remote copies, remote signals or barrier semaphores. Data moves between devices by JAX's collectives and lax.ppermute only.
A program may use at most 128 MiB of HBM per device.

v0:
```python
import math
import jax
import jax.numpy as jnp
from jax import lax
from jax.sharding import PartitionSpec as P

NLON = 1536
BLOCK = 128
HALO = 128


def extended_2(cells, sides, width):
    for axis, dim in sides:
        count = lax.axis_size(axis)
        head = lax.slice_in_dim(cells, 0, width, axis=dim)
        tail = lax.slice_in_dim(cells, cells.shape[dim] - width, cells.shape[dim], axis=dim)
        cells = jnp.concatenate(
            [
                lax.ppermute(tail, axis, [(i, (i + 1) % count) for i in range(count)]),
                cells,
                lax.ppermute(head, axis, [((i + 1) % count, i) for i in range(count)]),
            ],
            axis=dim,
        )
    return cells


def fourier_matrix(wave_count, longitude_count):
    wave_index = lax.broadcasted_iota(jnp.int32, (wave_count, longitude_count), 0)
    lon_index = lax.broadcasted_iota(jnp.int32, (wave_count, longitude_count), 1)
    angle_values = (wave_index * lon_index % longitude_count).astype(jnp.float32) * (
        2.0 * math.pi / longitude_count
    )
    factor = jnp.where(wave_index == 0, 1.0, 2.0).astype(jnp.float32)
    return jnp.stack(
        [factor * jnp.cos(angle_values), -factor * jnp.sin(angle_values)], axis=0
    ).astype(jnp.bfloat16)


def body(spectra, legendre, row_map, seg_map, interp, edges, inv_len):
    own_spectra = spectra[0]
    spectral = jnp.einsum(
        "mrj,mclj->lrcm",
        legendre,
        lax.all_gather(own_spectra, "lev", axis=2, tiled=True),
        preferred_element_type=jnp.float32,
    ).astype(jnp.bfloat16)
    banded = lax.all_to_all(
        lax.all_to_all(spectral, "lev", split_axis=0, concat_axis=1, tiled=True),
        "wave",
        split_axis=1,
        concat_axis=3,
        tiled=True,
    )
    fourier_modes = fourier_matrix(banded.shape[3], NLON)
    grid_field = jnp.einsum(
        "lrcm,cmk->lrk", banded, fourier_modes, preferred_element_type=jnp.float32
    ).astype(jnp.bfloat16)
    level_count = grid_field.shape[0]
    rows_dev = grid_field.shape[1]
    segments = NLON // BLOCK
    blocks_dev = row_map.shape[1]
    patch_count = lax.axis_size("wave")
    capacity = min(blocks_dev, max(3, 3 * blocks_dev // patch_count))
    own_band = lax.axis_index("wave")
    row_band = row_map // rows_dev
    is_mine = (row_band == own_band).astype(jnp.int32)
    slot_rank = jnp.cumsum(is_mine, axis=1) - is_mine
    slot_ids = jnp.arange(capacity, dtype=jnp.int32)
    slot_hit = (is_mine[:, :, None] == 1) & (slot_rank[:, :, None] == slot_ids[None, None, :])
    piece_index = row_map % rows_dev * segments + seg_map
    source_index = jnp.sum(jnp.where(slot_hit, piece_index[:, :, None], 0), axis=1)
    pieces = grid_field.reshape(level_count, rows_dev * segments, BLOCK)
    outgoing = jnp.take(pieces, source_index.reshape(-1), axis=1)
    incoming = lax.all_to_all(outgoing, "wave", split_axis=1, concat_axis=1, tiled=True)
    own_rows = lax.dynamic_index_in_dim(row_map, own_band, 0, keepdims=False)
    own_row_band = own_rows // rows_dev
    block_ids = jnp.arange(blocks_dev, dtype=jnp.int32)
    same_band = own_row_band[:, None] == own_row_band[None, :]
    earlier = block_ids[None, :] < block_ids[:, None]
    own_rank = jnp.sum((same_band & earlier).astype(jnp.int32), axis=1)
    arrival = own_row_band * capacity + own_rank
    gathered = jnp.take(incoming, arrival, axis=1)
    cell_field = jnp.einsum(
        "kij,lkj->lki", interp[0], gathered, preferred_element_type=jnp.float32
    ).astype(jnp.bfloat16)
    cell_field = cell_field.reshape(level_count, blocks_dev * BLOCK)
    extended = extended_2(cell_field, (("wave", 1),), HALO)
    edge_ids = edges[0]
    lengths = inv_len[0]
    pot_index = lax.axis_index("pot")
    first_cell = jnp.where(pot_index == 0, edge_ids[2], edge_ids[0])
    second_cell = jnp.where(pot_index == 0, edge_ids[3], edge_ids[1])
    weights_edge = jnp.where(pot_index == 0, -lengths[1], lengths[0])
    edge_term = (
        jnp.take(extended, second_cell, axis=1).astype(jnp.float32)
        - jnp.take(extended, first_cell, axis=1).astype(jnp.float32)
    ) * weights_edge
    normal_wind = lax.psum_scatter(edge_term, "pot", scatter_dimension=0, tiled=True).astype(
        jnp.bfloat16
    )
    return normal_wind


def solution(mesh):
    return jax.shard_map(
        body,
        mesh=mesh,
        in_specs=(
            P(("ens", "pot"), "wave", None, "lev", None),
            P("wave", "lev", None),
            P(),
            P(),
            P("wave", None, None, None),
            P("wave", None, None),
            P("wave", None, None),
        ),
        out_specs=P(("ens", "lev", "pot"), "wave"),
        check_vma=False,
    )
```

profile of v0, /device:TPU:0, one launch (start us, length us, event | category | flops | bytes accessed | tf_op | source)
XLA Modules:
  0.0 373.4 jit_solution(1620999810213235277)
XLA Ops:
  6.5 0.7 all-gather.3.cloned.1.call-update
  7.3 0.7 fusion.31
  9.3 0.7 bitcast_select_fusion.1
  10.2 2.2 broadcast_select_fusion.2
  12.3 32.4 %all-gather.3.cloned.1.call-done = bf16[1,16,2,64,512]{4,3,2,1,0:T(8,128)(2,1)} async-done(((bf16[1,16,2,32,512]{4,3,2,1,0:T(8,128)(2,1)}), bf16[1,16,2,64,512]{4,3,2,1,0:T(8,128)(2,1)}) %all-gather.3.cloned.1.call-update) | async-done | bytes 2097168 | tf_op jit(solution)/shard_map/all_gather | solution.py:45
  44.7 5.4 %fusion.8 = bf16[64,384,2,16]{1,0,2,3:T(8,128)(2,1)S(1)} fusion(bf16[16,384,512]{2,1,0:T(8,128)(2,1)} %param.10, bf16[1,16,2,64,512]{4,3,2,1,0:T(8,128)(2,1)} %all-gather.3.cloned.1.call-done), kind=kOutput, calls=%fused_computation.10 | convolution fusion | flops 806092800 | bytes 9961472 | tf_op jit(solution)/shard_map/mrj,mclj->lrcm/dot_general | solution.py:42
  50.1 2.8 copy.47
  52.9 3.7 all-to-all-start
  56.6 1.7 multiply_convert_fusion
  58.3 17.6 %all-to-all-done = bf16[64,384,2,16]{1,2,3,0:T(2,128)(2,1)S(1)} async-done(((bf16[64,384,2,16]{1,2,3,0:T(2,128)(2,1)}), bf16[64,384,2,16]{1,2,3,0:T(2,128)(2,1)S(1)}, u32[]{:S(2)}, u32[]{:S(2)}) %all-to-all-start) | async-done | bytes 1572896 | tf_op jit(solution)/shard_map/all_to_all | solution.py:49
  75.9 8.6 %copy.59 = bf16[32,2,384,2,16]{0,4,3,2,1:T(8,128)(2,1)} copy(bf16[32,2,384,2,16]{2,3,4,0,1:T(2,128)(2,1)S(1)} %bitcast.87) | data formatting | bytes 3145728 | tf_op jit(solution)/shard_map/all_to_all | solution.py:49
  84.5 8.3 %reshape.312 = bf16[4,2,98304]{2,1,0:T(2,128)(2,1)} reshape(bf16[768,2,16,32]{3,2,1,0:T(8,128)(2,1)} %bitcast.83) | data formatting | bytes 3145728
  92.8 4.7 %all-to-all-start.1 = ((bf16[4,2,98304]{2,1,0:T(2,128)(2,1)}), bf16[4,2,98304]{2,1,0:T(2,128)(2,1)S(1)}, u32[]{:S(2)}, u32[]{:S(2)}) async-start(bf16[4,2,98304]{2,1,0:T(2,128)(2,1)} %reshape.312), calls=%async_computation.1 | async-start | bytes 3145728 | tf_op jit(solution)/shard_map/all_to_all | solution.py:48
  98.2 35.2 %all-to-all-done.1 = bf16[4,2,98304]{2,1,0:T(2,128)(2,1)S(1)} async-done(((bf16[4,2,98304]{2,1,0:T(2,128)(2,1)}), bf16[4,2,98304]{2,1,0:T(2,128)(2,1)S(1)}, u32[]{:S(2)}, u32[]{:S(2)}) %all-to-all-start.1) | async-done | bytes 1572896 | tf_op jit(solution)/shard_map/all_to_all | solution.py:48
  133.5 4.6 %reshape.313 = bf16[768,2,16,32]{3,2,1,0:T(8,128)(2,1)} reshape(bf16[4,2,98304]{2,1,0:T(2,128)(2,1)S(1)} %all-to-all-done.1) | data formatting | bytes 3145728
  138.1 10.1 %copy.60 = bf16[32,4,192,2,16]{2,1,4,3,0:T(4,128)(2,1)S(1)} copy(bf16[32,4,192,2,16]{0,4,3,2,1:T(8,128)(2,1)} %bitcast.84) | data formatting | bytes 3145728 | tf_op jit(solution)/shard_map/all_to_all | solution.py:48
  148.7 9.1 %bitcast_convert_fusion = bf16[32,192,1536]{2,1,0:T(8,128)(2,1)} fusion(bf16[32,192,2,64]{1,3,2,0:T(8,128)(2,1)S(1)} %bitcast.85, bf16[1,64,1536]{2,1,0:T(8,128)(2,1)S(1)} %get-tuple-element.15, bf16[1,64,1536]{2,1,0:T(8,128)(2,1)S(1)} %get-tuple-element.16), kind=kOutput, calls=%fused_computation.4 | convolution fusion | flops 2425552896 | bytes 20840448 | tf_op jit(solution)/shard_map/lrcm,cmk->lrk/dot_general | solution.py:56
  157.8 35.2 %reshape.265 = bf16[32,2304,128]{2,1,0:T(8,128)(2,1)} reshape(bf16[32,192,1536]{2,1,0:T(8,128)(2,1)} %bitcast_convert_fusion) | data formatting | bytes 37748736 | tf_op jit(solution)/shard_map/reshape | solution.py:73
  193.0 20.7 %copy.52 = bf16[32,2304,128]{2,0,1:T(8,128)(2,1)} copy(bf16[32,2304,128]{2,1,0:T(8,128)(2,1)} %reshape.265) | data formatting | bytes 37748736 | tf_op jit(solution)/shard_map/reshape | solution.py:73
  213.7 7.1 %gather_fusion = bf16[96,32,128]{2,1,0:T(8,128)(2,1)S(1)} fusion(bf16[32,2304,128]{2,0,1:T(8,128)(2,1)} %copy.52, s32[1024]{0:T(1024)S(1)} %pad_clamp_fusion.1), kind=kCustom, calls=%fused_computation.2 | custom fusion | bytes 1573248 | tf_op jit(solution)/shard_map/jit(_take)/gather | solution.py:74
  220.8 1.1 select_bitcast_fusion
  221.9 3.5 all-to-all-start.2
  225.6 19.5 %all-to-all-done.2 = bf16[32,96,128]{2,0,1:T(8,128)(2,1)S(1)} async-done(((bf16[32,96,128]{2,0,1:T(8,128)(2,1)}), bf16[32,96,128]{2,0,1:T(8,128)(2,1)S(1)}, u32[]{:S(2)}, u32[]{:S(2)}) %all-to-all-start.2) | async-done | bytes 786464 | tf_op jit(solution)/shard_map/all_to_all | solution.py:75
  246.4 1.5 collective-permute-start.1
  248.5 1.6 collective-permute-done.1
  250.1 3.3 collective-permute-done
  253.9 43.3 %gather_fusion.3 = bf16[12288,32]{1,0:T(8,128)(2,1)} fusion(bf16[32,4352]{0,1:T(8,128)(2,1)S(1)} %copy.54, s32[12288]{0:T(1024)S(1)} %fusion.28), kind=kCustom, calls=%fused_computation.1.clone | custom fusion | bytes 1622016 | tf_op jit(solution)/shard_map/jit(_take)/gather | solution.py:97
  297.3 43.3 %gather_fusion.2 = bf16[12288,32]{1,0:T(8,128)(2,1)} fusion(bf16[32,4352]{0,1:T(8,128)(2,1)S(1)} %copy.54, s32[12288]{0:T(1024)S(1)} %fusion.27), kind=kCustom, calls=%fused_computation.clone | custom fusion | bytes 1622016 | tf_op jit(solution)/shard_map/jit(_take)/gather | solution.py:96
  340.5 12.1 %subtract_multiply_fusion = f32[32,12288]{0,1:T(8,128)} fusion(bf16[12288,32]{1,0:T(8,128)(2,1)} %gather_fusion.3, bf16[12288,32]{1,0:T(8,128)(2,1)} %gather_fusion.2, f32[12288]{0:T(1024)S(1)} %bitcast.94, pred[12288]{0:T(1024)(128)(4,1)S(1)} %get-tuple-element.17, pred[12288]{0:T(1024)(128)(4,1)S(1)} %get-tuple-element.18), kind=kLoop, calls=%fused_computation.7 | loop fusion | flops 2359296 | bytes 3219456 | tf_op jit(solution)/shard_map/mul | solution.py:95
  352.6 5.5 %copy.61 = f32[32,12288]{1,0:T(8,128)} copy(f32[32,12288]{0,1:T(8,128)} %subtract_multiply_fusion) | data formatting | bytes 3145728
  358.2 6.4 %reduce-scatter.4.cloned.1.call-done = f32[16,12288]{1,0:T(8,128)} async-done(((f32[32,12288]{1,0:T(8,128)}), f32[16,12288]{1,0:T(8,128)}) %reduce-scatter.4.cloned.1.call-update) | async-done | bytes 786448 | tf_op jit(solution)/shard_map/reduce_scatter | solution.py:99
  364.6 1.9 convert_element_type.57
  (45 shorter events, 5.2 us)
Async XLA Ops:
  6.5 239.1 %copy-start = (bf16[1,32,128,128]{3,2,1,0:T(8,128)(2,1)S(1)}, bf16[1,32,128,128]{3,2,1,0:T(8,128)(2,1)}, u32[]{:S(2)}) copy-start(bf16[1,32,128,128]{3,2,1,0:T(8,128)(2,1)} %param.13) | copy-start | bytes 3145732
  6.5 38.2 %all-gather.3.cloned.1.call-start = ((), (), s32[]{:S(2)}) async-start(), calls=%async_computation.4 | async-start | bytes 3145728 | tf_op jit(solution)/shard_map/all_gather | solution.py:45
  10.2 46.4 %copy-start.5 = (s32[32]{0:T(128)}, s32[32]{0:T(128)S(1)}, u32[]{:S(2)}) copy-start(s32[32]{0:T(128)S(1)} %convert_reduce_fusion) | copy-start | bytes 388
  52.9 23.0 %all-to-all-start = ((bf16[64,384,2,16]{1,2,3,0:T(2,128)(2,1)}), bf16[64,384,2,16]{1,2,3,0:T(2,128)(2,1)S(1)}, u32[]{:S(2)}, u32[]{:S(2)}) async-start(bf16[64,384,2,16]{1,2,3,0:T(2,128)(2,1)} %copy.47), calls=%async_computation | async-start | bytes 3145728 | tf_op jit(solution)/shard_map/all_to_all | solution.py:49
  92.8 4.7 %copy-start.4 = (f32[1,2,12288]{2,1,0:T(2,128)S(1)}, f32[1,2,12288]{2,1,0:T(2,128)}, u32[]{:S(2)}) copy-start(f32[1,2,12288]{2,1,0:T(2,128)} %param.15) | copy-start | bytes 294916
  92.8 40.7 %all-to-all-start.1 = ((bf16[4,2,98304]{2,1,0:T(2,128)(2,1)}), bf16[4,2,98304]{2,1,0:T(2,128)(2,1)S(1)}, u32[]{:S(2)}, u32[]{:S(2)}) async-start(bf16[4,2,98304]{2,1,0:T(2,128)(2,1)} %reshape.312), calls=%async_computation.1 | async-start | bytes 3145728 | tf_op jit(solution)/shard_map/all_to_all | solution.py:48
  213.7 11.7 %copy-start.6 = (s32[32]{0:T(128)S(1)}, s32[32]{0:T(128)}, u32[]{:S(2)}) copy-start(s32[32]{0:T(128)} %copy-done.5) | copy-start | bytes 388
  213.7 11.8 %copy-start.2 = (s32[1,1,12288]{2,1,0:T(1,128)S(1)}, s32[1,1,12288]{2,1,0:T(1,128)}, u32[]{:S(2)}) copy-start(s32[1,1,12288]{2,1,0:T(1,128)} %get-tuple-element.14) | copy-start | bytes 147460
  213.7 11.8 %copy-start.1 = (s32[1,1,12288]{2,1,0:T(1,128)S(1)}, s32[1,1,12288]{2,1,0:T(1,128)}, u32[]{:S(2)}) copy-start(s32[1,1,12288]{2,1,0:T(1,128)} %get-tuple-element.13) | copy-start | bytes 147460
  221.9 23.1 %all-to-all-start.2 = ((bf16[32,96,128]{2,0,1:T(8,128)(2,1)}), bf16[32,96,128]{2,0,1:T(8,128)(2,1)S(1)}, u32[]{:S(2)}, u32[]{:S(2)}) async-start(bf16[32,96,128]{2,0,1:T(8,128)(2,1)} %select_bitcast_fusion), calls=%async_computation.2 | async-start | bytes 1572864 | tf_op jit(solution)/shard_map/all_to_all | solution.py:75
  225.4 139.2 %reduce-scatter.4.cloned.1.call-start = ((), (), s32[]{:S(2)}) async-start(), calls=%async_computation.5 | async-start | bytes 2359296 | tf_op jit(solution)/shard_map/reduce_scatter | solution.py:99
  246.4 3.7 collective-permute-start.1
  247.9 5.4 %collective-permute-start = (bf16[32,128]{1,0:T(8,128)(2,1)S(1)}, bf16[32,128]{1,0:T(8,128)(2,1)S(1)}, u32[]{:S(2)}, u32[]{:S(2)}) collective-permute-start(bf16[32,128]{1,0:T(8,128)(2,1)S(1)} %get-tuple-element.11), channel_id=1, source_target_pairs={{0,4},{4,8},{8,12},{12,0},{1,5},{5,9},{9,13},{13,1},{2,6},{6,10},{... | collective-permute-start | bytes 24584 | tf_op jit(solution)/shard_map/ppermute | solution.py:19
  297.3 43.3 %copy-start.3 = (f32[1,1,12288]{2,1,0:T(1,128)S(1)}, f32[1,1,12288]{2,1,0:T(1,128)}, u32[]{:S(2)}) copy-start(f32[1,1,12288]{2,1,0:T(1,128)} %broadcast_select_fusion) | copy-start | bytes 147460
Sparse Core Ops, SparseCore 0:
  8.9 35.8 all-gather.2
  358.3 6.2 reduce-scatter.3
where the time goes:
time: 375 us; the launch traced here: 373 us
  local copies, waits for them, and re-layouts  191 us (51%)
  waiting for transfers between devices  117 us (31%)
  other arithmetic  22.4 us (6%)
  matrix products  15.2 us (4%)
  starting transfers between devices  14 us (4%)
  between operations  13.6 us (4%)
    reshape x2, local copies, waits for them, and re-layouts, body(): pieces = grid_field.reshape(level_count, rows_dev * segments, BLOCK)  55.9 us
    gather x1, local copies, waits for them, and re-layouts, body(): jnp.take(extended, first_cell, axis=1).astype(jnp.float32)  43.3 us
    gather x1, local copies, waits for them, and re-layouts, body(): jnp.take(extended, second_cell, axis=1).astype(jnp.float32)  43.3 us
    all_to_all x1, waiting for transfers between devices, body(): lax.all_to_all(lax.all_to_all(spectral, 'lev', split_axis=0, concat_axis=...  35.2 us
    all_gather x1, waiting for transfers between devices, body(): lax.all_gather(own_spectra, 'lev', axis=2, tiled=True)  32.4 us
    all_to_all x1, waiting for transfers between devices, body(): lax.all_to_all(outgoing, 'wave', split_axis=1, concat_axis=1, tiled=True)  19.5 us
    unnamed x17, local copies, waits for them, and re-layouts  18.5 us
    all_to_all x1, waiting for transfers between devices, body(): lax.all_to_all(spectral, 'lev', split_axis=0, concat_axis=1, tiled=True)  17.6 us
  transfers between devices with their start and end apart: 7, of which 7 were waited for; matrix products, arithmetic and copies ran while one was open for 2% of the time, Pallas kernels for 0%

commit v1 on v0

--- a/solution.py
+++ b/solution.py
@@ -7,6 +7,21 @@
 NLON = 1536
 BLOCK = 128
 HALO = 128
+
+
+def ring_apply(value, axis, dim, make, out_dim):
+    ways, here, step = (lax.axis_size(axis), lax.axis_index(axis), value.shape[dim])
+    results = []
+    for far in range(ways):
+        arriving = (
+            lax.ppermute(value, axis, [(d, (d + 1) % ways) for d in range(ways)])
+            if far + 1 < ways
+            else value
+        )
+        results.append(make(value, (here - far) % ways * step))
+        value = arriving
+    line = jnp.concatenate(results[::-1], axis=out_dim)
+    return jnp.roll(line, (here + 1) * results[0].shape[out_dim], axis=out_dim)
 
 
 def extended_2(cells, sides, width):
@@ -39,11 +54,14 @@
 
 def body(spectra, legendre, row_map, seg_map, interp, edges, inv_len):
     own_spectra = spectra[0]
-    spectral = jnp.einsum(
-        "mrj,mclj->lrcm",
-        legendre,
-        lax.all_gather(own_spectra, "lev", axis=2, tiled=True),
-        preferred_element_type=jnp.float32,
+    spectral = ring_apply(
+        own_spectra,
+        "lev",
+        2,
+        lambda part, offset: jnp.einsum(
+            "mrj,mclj->lrcm", legendre, part, preferred_element_type=jnp.float32
+        ),
+        0,
     ).astype(jnp.bfloat16)
     banded = lax.all_to_all(
         lax.all_to_all(spectral, "lev", split_axis=0, concat_axis=1, tiled=True),

time: 375 us -> 363 us (0.968)
  waiting for transfers between devices: 117 us -> 94.2 us
  starting transfers between devices: 14 us -> 19 us
    all_gather x1 -> x0, waiting for transfers between devices: 32.4 us -> none  [body(): lax.all_gather(own_spectra, 'lev', axis=2, tiled=True)]
    ppermute x0 -> x1, waiting for transfers between devices: none -> 11.5 us  [ring_apply(): lax.ppermute(value, axis, [(d, (d + 1) % ways) for d in range(ways)])]
    unnamed x17 -> x19, local copies, waits for them, and re-layouts: 18.5 us -> 18.5 us
  transfers between devices with their start and end apart: 7 -> 7, of which waited for: 7 -> 6; matrix products, arithmetic and copies ran while one was open for 2% -> 4% of each run, Pallas kernels for 0% -> 0%
where the time goes in v1:
time: 363 us; the launch traced here: 361 us
  local copies, waits for them, and re-layouts  192 us (53%)
  waiting for transfers between devices  94.2 us (26%)
  other arithmetic  25.1 us (7%)
  starting transfers between devices  19 us (5%)
  matrix products  17.1 us (5%)
  between operations  13.6 us (4%)
    reshape x2, local copies, waits for them, and re-layouts, body(): pieces = grid_field.reshape(level_count, rows_dev * segments, BLOCK)  55.9 us
    gather x1, local copies, waits for them, and re-layouts, body(): jnp.take(extended, second_cell, axis=1).astype(jnp.float32)  43.6 us
    gather x1, local copies, waits for them, and re-layouts, body(): jnp.take(extended, first_cell, axis=1).astype(jnp.float32)  43.6 us
    all_to_all x1, waiting for transfers between devices, body(): lax.all_to_all(lax.all_to_all(spectral, 'lev', split_axis=0, concat_axis=...  34.6 us
    all_to_all x1, waiting for transfers between devices, body(): lax.all_to_all(outgoing, 'wave', split_axis=1, concat_axis=1, tiled=True)  19.5 us
    unnamed x19, local copies, waits for them, and re-layouts  18.5 us
    all_to_all x1, waiting for transfers between devices, body(): lax.all_to_all(spectral, 'lev', split_axis=0, concat_axis=1, tiled=True)  17.3 us
    mul x1, other arithmetic, body(): (jnp.take(extended, second_cell, axis=1).astype(jnp.float32) - jnp.take(e...  12.1 us
  transfers between devices with their start and end apart: 7, of which 6 were waited for; matrix products, arithmetic and copies ran while one was open for 4% of the time, Pallas kernels for 0%

profile of v1, /device:TPU:0, one launch (start us, length us, event | category | flops | bytes accessed | tf_op | source)
XLA Modules:
  0.0 361.3 jit_solution(5306546601771904322)
XLA Ops:
  6.5 3.0 collective-permute-start
  12.2 2.2 broadcast_select_fusion.2
  14.5 1.5 multiply_convert_fusion
  16.1 5.3 %fusion.11 = bf16[32,384,2,16]{1,0,2,3:T(8,128)(2,1)S(1)} fusion(bf16[16,384,512]{2,1,0:T(8,128)(2,1)} %param.10, bf16[1,16,2,32,512]{4,3,2,1,0:T(8,128)(2,1)} %param.9), kind=kOutput, calls=%fused_computation.19 | convolution fusion | flops 402653184 | bytes 8126464 | tf_op jit(solution)/shard_map/mrj,mclj->lrcm/dot_general | solution.py:61
  21.4 11.5 %collective-permute-done = bf16[16,2,32,512]{3,2,1,0:T(8,128)(2,1)S(1)} collective-permute-done((bf16[16,2,32,512]{3,2,1,0:T(8,128)(2,1)}, bf16[16,2,32,512]{3,2,1,0:T(8,128)(2,1)S(1)}, u32[]{:S(2)}, u32[]{:S(2)}) %collective-permute-start) | collective-permute-done | bytes 1048608 | tf_op jit(solution)/shard_map/ppermute | solution.py:17
  32.9 2.0 fusion.8
  34.9 1.4 fusion.7
  36.3 2.8 copy.47
  39.1 3.7 %all-to-all-start = ((bf16[64,384,2,16]{1,2,3,0:T(2,128)(2,1)}), bf16[64,384,2,16]{1,2,3,0:T(2,128)(2,1)S(1)}, u32[]{:S(2)}, u32[]{:S(2)}) async-start(bf16[64,384,2,16]{1,2,3,0:T(2,128)(2,1)} %copy.47), calls=%async_computation | async-start | bytes 3145728 | tf_op jit(solution)/shard_map/all_to_all | solution.py:67
  42.8 1.5 multiply_convert_fusion.1
  44.3 17.3 %all-to-all-done = bf16[64,384,2,16]{1,2,3,0:T(2,128)(2,1)S(1)} async-done(((bf16[64,384,2,16]{1,2,3,0:T(2,128)(2,1)}), bf16[64,384,2,16]{1,2,3,0:T(2,128)(2,1)S(1)}, u32[]{:S(2)}, u32[]{:S(2)}) %all-to-all-start) | async-done | bytes 1572896 | tf_op jit(solution)/shard_map/all_to_all | solution.py:67
  61.6 8.7 %copy.59 = bf16[32,2,384,2,16]{0,4,3,2,1:T(8,128)(2,1)} copy(bf16[32,2,384,2,16]{2,3,4,0,1:T(2,128)(2,1)S(1)} %bitcast.88) | data formatting | bytes 3145728 | tf_op jit(solution)/shard_map/all_to_all | solution.py:67
  70.3 8.3 %reshape.311 = bf16[4,2,98304]{2,1,0:T(2,128)(2,1)} reshape(bf16[768,2,16,32]{3,2,1,0:T(8,128)(2,1)} %bitcast.84) | data formatting | bytes 3145728
  78.6 5.0 %all-to-all-start.1 = ((bf16[4,2,98304]{2,1,0:T(2,128)(2,1)}), bf16[4,2,98304]{2,1,0:T(2,128)(2,1)S(1)}, u32[]{:S(2)}, u32[]{:S(2)}) async-start(bf16[4,2,98304]{2,1,0:T(2,128)(2,1)} %reshape.311), calls=%async_computation.1 | async-start | bytes 3145728 | tf_op jit(solution)/shard_map/all_to_all | solution.py:66
  84.3 34.6 %all-to-all-done.1 = bf16[4,2,98304]{2,1,0:T(2,128)(2,1)S(1)} async-done(((bf16[4,2,98304]{2,1,0:T(2,128)(2,1)}), bf16[4,2,98304]{2,1,0:T(2,128)(2,1)S(1)}, u32[]{:S(2)}, u32[]{:S(2)}) %all-to-all-start.1) | async-done | bytes 1572896 | tf_op jit(solution)/shard_map/all_to_all | solution.py:66
  118.8 4.6 %reshape.312 = bf16[768,2,16,32]{3,2,1,0:T(8,128)(2,1)} reshape(bf16[4,2,98304]{2,1,0:T(2,128)(2,1)S(1)} %all-to-all-done.1) | data formatting | bytes 3145728
  123.5 10.1 %copy.60 = bf16[32,4,192,2,16]{2,1,4,3,0:T(4,128)(2,1)S(1)} copy(bf16[32,4,192,2,16]{0,4,3,2,1:T(8,128)(2,1)} %bitcast.85) | data formatting | bytes 3145728 | tf_op jit(solution)/shard_map/all_to_all | solution.py:66
  134.1 9.1 %bitcast_convert_fusion = bf16[32,192,1536]{2,1,0:T(8,128)(2,1)} fusion(bf16[32,192,2,64]{1,3,2,0:T(8,128)(2,1)S(1)} %bitcast.86, bf16[1,64,1536]{2,1,0:T(8,128)(2,1)S(1)} %multiply_convert_fusion, bf16[1,64,1536]{2,1,0:T(8,128)(2,1)S(1)} %multiply_convert_fusion.1), kind=kOutput, calls=%fused_computation.4 | convolution fusion | flops 2425552896 | bytes 20840448 | tf_op jit(solution)/shard_map/lrcm,cmk->lrk/dot_general | solution.py:74
  143.2 35.2 %reshape.265 = bf16[32,2304,128]{2,1,0:T(8,128)(2,1)} reshape(bf16[32,192,1536]{2,1,0:T(8,128)(2,1)} %bitcast_convert_fusion) | data formatting | bytes 37748736 | tf_op jit(solution)/shard_map/reshape | solution.py:91
  178.4 20.7 %copy.52 = bf16[32,2304,128]{2,0,1:T(8,128)(2,1)} copy(bf16[32,2304,128]{2,1,0:T(8,128)(2,1)} %reshape.265) | data formatting | bytes 37748736 | tf_op jit(solution)/shard_map/reshape | solution.py:91
  199.1 7.1 %gather_fusion = bf16[96,32,128]{2,1,0:T(8,128)(2,1)S(1)} fusion(bf16[32,2304,128]{2,0,1:T(8,128)(2,1)} %copy.52, s32[1024]{0:T(1024)S(1)} %pad_clamp_fusion.1), kind=kCustom, calls=%fused_computation.2 | custom fusion | bytes 1573248 | tf_op jit(solution)/shard_map/jit(_take)/gather | solution.py:92
  206.2 1.1 select_bitcast_fusion
  207.3 3.5 all-to-all-start.2
  211.0 19.5 %all-to-all-done.2 = bf16[32,96,128]{2,0,1:T(8,128)(2,1)S(1)} async-done(((bf16[32,96,128]{2,0,1:T(8,128)(2,1)}), bf16[32,96,128]{2,0,1:T(8,128)(2,1)S(1)}, u32[]{:S(2)}, u32[]{:S(2)}) %all-to-all-start.2) | async-done | bytes 786464 | tf_op jit(solution)/shard_map/all_to_all | solution.py:93
  231.9 3.8 %collective-permute-start.2 = (bf16[32,128]{1,0:T(8,128)(2,1)S(1)}, bf16[32,128]{1,0:T(8,128)(2,1)S(1)}, u32[]{:S(2)}, u32[]{:S(2)}) collective-permute-start(bf16[32,128]{1,0:T(8,128)(2,1)S(1)} %get-tuple-element.12), channel_id=1, source_target_pairs={{4,0},{8,4},{12,8},{0,12},{5,1},{9,5},{13,9},{1,13},{6,2},{10,6},{... | collective-permute-start | bytes 24584 | tf_op jit(solution)/shard_map/ppermute | solution.py:36
  235.7 1.6 collective-permute-done.1
  237.9 43.6 %gather_fusion.2 = bf16[12288,32]{1,0:T(8,128)(2,1)} fusion(bf16[32,4352]{0,1:T(8,128)(2,1)S(1)} %copy.54, s32[12288]{0:T(1024)S(1)} %fusion.28), kind=kCustom, calls=%fused_computation.clone | custom fusion | bytes 1622016 | tf_op jit(solution)/shard_map/jit(_take)/gather | solution.py:114
  281.5 43.6 %gather_fusion.3 = bf16[12288,32]{1,0:T(8,128)(2,1)} fusion(bf16[32,4352]{0,1:T(8,128)(2,1)S(1)} %copy.54, s32[12288]{0:T(1024)S(1)} %fusion.29), kind=kCustom, calls=%fused_computation.1.clone | custom fusion | bytes 1622016 | tf_op jit(solution)/shard_map/jit(_take)/gather | solution.py:115
  325.1 12.1 %subtract_multiply_fusion = f32[32,12288]{0,1:T(8,128)} fusion(bf16[12288,32]{1,0:T(8,128)(2,1)} %gather_fusion.3, bf16[12288,32]{1,0:T(8,128)(2,1)} %gather_fusion.2, f32[12288]{0:T(1024)S(1)} %bitcast.96, pred[12288]{0:T(1024)(128)(4,1)S(1)} %get-tuple-element.17, pred[12288]{0:T(1024)(128)(4,1)S(1)} %get-tuple-element.18), kind=kLoop, calls=%fused_computation.13 | loop fusion | flops 2359296 | bytes 3219456 | tf_op jit(solution)/shard_map/mul | solution.py:113
  337.2 5.6 %copy.61 = f32[32,12288]{1,0:T(8,128)} copy(f32[32,12288]{0,1:T(8,128)} %subtract_multiply_fusion) | data formatting | bytes 3145728
  342.8 9.8 %reduce-scatter.4.cloned.1.call-done = f32[16,12288]{1,0:T(8,128)} async-done(((f32[32,12288]{1,0:T(8,128)}), f32[16,12288]{1,0:T(8,128)}) %reduce-scatter.4.cloned.1.call-update) | async-done | bytes 786448 | tf_op jit(solution)/shard_map/reduce_scatter | solution.py:117
  352.6 1.9 convert_element_type.53
  (48 shorter events, 6.1 us)
Async XLA Ops:
  6.5 224.5 %copy-start = (bf16[1,32,128,128]{3,2,1,0:T(8,128)(2,1)S(1)}, bf16[1,32,128,128]{3,2,1,0:T(8,128)(2,1)}, u32[]{:S(2)}) copy-start(bf16[1,32,128,128]{3,2,1,0:T(8,128)(2,1)} %param.13) | copy-start | bytes 3145732
  6.5 26.3 %collective-permute-start = (bf16[16,2,32,512]{3,2,1,0:T(8,128)(2,1)}, bf16[16,2,32,512]{3,2,1,0:T(8,128)(2,1)S(1)}, u32[]{:S(2)}, u32[]{:S(2)}) collective-permute-start(bf16[16,2,32,512]{3,2,1,0:T(8,128)(2,1)} %bitcast.91), channel_id=1, source_target_pairs={{0,2},{2,0},{1,3},{3,1},{4,6},{6,4},{5,7},{7,5},{8,10},{10,8},{9,1... | collective-permute-start | bytes 3145736 | tf_op jit(solution)/shard_map/ppermute | solution.py:17
  14.5 28.2 %copy-start.6 = (s32[32]{0:T(128)}, s32[32]{0:T(128)S(1)}, u32[]{:S(2)}) copy-start(s32[32]{0:T(128)S(1)} %convert_reduce_fusion) | copy-start | bytes 388
  16.1 16.8 %copy-start.1 = (bf16[16,384,512]{2,1,0:T(8,128)(2,1)S(1)}, bf16[16,384,512]{2,1,0:T(8,128)(2,1)}, u32[]{:S(2)}) copy-start(bf16[16,384,512]{2,1,0:T(8,128)(2,1)} %param.10) | copy-start | bytes 18874372
  39.1 22.6 %all-to-all-start = ((bf16[64,384,2,16]{1,2,3,0:T(2,128)(2,1)}), bf16[64,384,2,16]{1,2,3,0:T(2,128)(2,1)S(1)}, u32[]{:S(2)}, u32[]{:S(2)}) async-start(bf16[64,384,2,16]{1,2,3,0:T(2,128)(2,1)} %copy.47), calls=%async_computation | async-start | bytes 3145728 | tf_op jit(solution)/shard_map/all_to_all | solution.py:67
  78.6 5.0 %copy-start.5 = (f32[1,2,12288]{2,1,0:T(2,128)S(1)}, f32[1,2,12288]{2,1,0:T(2,128)}, u32[]{:S(2)}) copy-start(f32[1,2,12288]{2,1,0:T(2,128)} %param.15) | copy-start | bytes 294916
  78.6 40.2 %all-to-all-start.1 = ((bf16[4,2,98304]{2,1,0:T(2,128)(2,1)}), bf16[4,2,98304]{2,1,0:T(2,128)(2,1)S(1)}, u32[]{:S(2)}, u32[]{:S(2)}) async-start(bf16[4,2,98304]{2,1,0:T(2,128)(2,1)} %reshape.311), calls=%async_computation.1 | async-start | bytes 3145728 | tf_op jit(solution)/shard_map/all_to_all | solution.py:66
  199.1 11.7 %copy-start.7 = (s32[32]{0:T(128)S(1)}, s32[32]{0:T(128)}, u32[]{:S(2)}) copy-start(s32[32]{0:T(128)} %copy-done.6) | copy-start | bytes 388
  199.1 11.8 %copy-start.3 = (s32[1,1,12288]{2,1,0:T(1,128)S(1)}, s32[1,1,12288]{2,1,0:T(1,128)}, u32[]{:S(2)}) copy-start(s32[1,1,12288]{2,1,0:T(1,128)} %get-tuple-element.13) | copy-start | bytes 147460
  199.1 11.8 %copy-start.2 = (s32[1,1,12288]{2,1,0:T(1,128)S(1)}, s32[1,1,12288]{2,1,0:T(1,128)}, u32[]{:S(2)}) copy-start(s32[1,1,12288]{2,1,0:T(1,128)} %get-tuple-element.14) | copy-start | bytes 147460
  207.3 23.1 %all-to-all-start.2 = ((bf16[32,96,128]{2,0,1:T(8,128)(2,1)}), bf16[32,96,128]{2,0,1:T(8,128)(2,1)S(1)}, u32[]{:S(2)}, u32[]{:S(2)}) async-start(bf16[32,96,128]{2,0,1:T(8,128)(2,1)} %select_bitcast_fusion), calls=%async_computation.2 | async-start | bytes 1572864 | tf_op jit(solution)/shard_map/all_to_all | solution.py:93
  210.8 141.8 %reduce-scatter.4.cloned.1.call-start = ((), (), s32[]{:S(2)}) async-start(), calls=%async_computation.4 | async-start | bytes 2359296 | tf_op jit(solution)/shard_map/reduce_scatter | solution.py:117
  231.8 5.5 %collective-permute-start.1 = (bf16[32,128]{1,0:T(8,128)(2,1)S(1)}, bf16[32,128]{1,0:T(8,128)(2,1)S(1)}, u32[]{:S(2)}, u32[]{:S(2)}) collective-permute-start(bf16[32,128]{1,0:T(8,128)(2,1)S(1)} %get-tuple-element.11), channel_id=1, source_target_pairs={{0,4},{4,8},{8,12},{12,0},{1,5},{5,9},{9,13},{13,1},{2,6},{6,10},{... | collective-permute-start | bytes 24584 | tf_op jit(solution)/shard_map/ppermute | solution.py:34
  231.9 5.4 %collective-permute-start.2 = (bf16[32,128]{1,0:T(8,128)(2,1)S(1)}, bf16[32,128]{1,0:T(8,128)(2,1)S(1)}, u32[]{:S(2)}, u32[]{:S(2)}) collective-permute-start(bf16[32,128]{1,0:T(8,128)(2,1)S(1)} %get-tuple-element.12), channel_id=1, source_target_pairs={{4,0},{8,4},{12,8},{0,12},{5,1},{9,5},{13,9},{1,13},{6,2},{10,6},{... | collective-permute-start | bytes 24584 | tf_op jit(solution)/shard_map/ppermute | solution.py:36
  281.5 43.6 %copy-start.4 = (f32[1,1,12288]{2,1,0:T(1,128)S(1)}, f32[1,1,12288]{2,1,0:T(1,128)}, u32[]{:S(2)}) copy-start(f32[1,1,12288]{2,1,0:T(1,128)} %broadcast_select_fusion) | copy-start | bytes 147460
Sparse Core Ops, SparseCore 0:
  342.9 9.5 reduce-scatter.3
